TPU v7x, 256 devices: a whole 4x4x8 slice. The times are simulated.
256 devices in a mesh: frame: 8 (over z), tile: 32 (over x, y, core).
Axes of the slice: x: 4, y: 4, z: 8, core: 2. Of those that a mesh axis runs over, the one named last changes fastest.
Arguments:
- displacement: bfloat16 [512, 2, 32, 4096], P('frame', None, 'tile'), may hold values from -256 to 256
Outputs:
- basis: bfloat16 [512, 3, 32, 4096], P(None, None, 'tile', 'frame')
- factor: float32 [512, 512], replicated
All inputs are finite; a program needn't handle non-finite values.
Results may differ from a plain program's by a relative error of at most 0.0053.
The roundings to bfloat16 on the way count: a program that leaves them out, or rounds other values in their place, can miss the bound.
Values may be sent and summed in bfloat16 or wider, within the bound.
No kernel may reach another device: no remote copies, remote signals or barrier semaphores. Data moves between devices by JAX's collectives and lax.ppermute only.
A program may use at most 64 MiB of HBM per device.

v0:
```python
import math
import jax
import jax.numpy as jnp
from jax import lax
from jax.sharding import PartitionSpec as P


def with_halo(array, sides, width):
    for axis, dim in sides:
        peers, length = (lax.axis_size(axis), array.shape[dim])
        up = [(i, (i + 1) % peers) for i in range(peers - 1)]
        down = [(j, i) for i, j in up]
        last = lax.slice_in_dim(array, length - width, length, axis=dim)
        first = lax.slice_in_dim(array, 0, width, axis=dim)
        before = lax.ppermute(last, axis, up)
        after = lax.ppermute(first, axis, down)
        array = jnp.concatenate([before, array, after], axis=dim)
    return array


def derivative(center, before, after, first, final):
    return jnp.where(
        first, after - center, jnp.where(final, center - before, (after - before) * 0.5)
    )


def column_derivative(center):
    width = center.shape[-1]
    after = jnp.concatenate([center[..., 1:], center[..., -1:]], axis=-1)
    before = jnp.concatenate([center[..., :1], center[..., :-1]], axis=-1)
    column = jnp.arange(width, dtype=jnp.int32)
    return derivative(center, before, after, column == 0, column == width - 1)


def combine_strain(d_rows, d_cols):
    return jnp.stack(
        [d_cols[:, 0], d_rows[:, 1], 0.5 * (d_rows[:, 0] + d_cols[:, 1])], axis=1
    ).astype(jnp.bfloat16)


def local(displacement):
    rows = displacement.shape[2]
    full_width = displacement.shape[3]
    total_rows = lax.axis_size("tile") * rows
    scale = math.sqrt(3 * total_rows * full_width)
    row_global = lax.axis_index("tile") * rows + jnp.arange(rows, dtype=jnp.int32)
    first = (row_global == 0)[:, None]
    final = (row_global == total_rows - 1)[:, None]
    padded = with_halo(displacement, (("tile", 2),), 1)
    field = padded.astype(jnp.float32)
    center = field[:, :, 1:-1, :]
    d_rows = derivative(center, field[:, :, :-2, :], field[:, :, 2:, :], first, final)
    d_cols = column_derivative(center)
    strain = combine_strain(d_rows, d_cols)
    pixel_major = lax.all_to_all(strain, "frame", split_axis=3, concat_axis=0, tiled=True)
    frames = pixel_major.shape[0]
    snapshot_half = pixel_major.reshape(frames, -1)
    local_gram = lax.dot_general(
        snapshot_half, snapshot_half, (((1,), (1,)), ((), ())), preferred_element_type=jnp.float32
    )
    gram = lax.psum(local_gram, ("frame", "tile"))
    lower = jnp.linalg.cholesky(gram)
    snapshot = snapshot_half.astype(jnp.float32)
    solved = lax.linalg.triangular_solve(lower, snapshot, left_side=True, lower=True)
    basis = (solved * scale).astype(jnp.bfloat16).reshape(pixel_major.shape)
    return (basis, lower.T / scale)


def solution(mesh):
    return jax.shard_map(
        local,
        mesh=mesh,
        in_specs=(P("frame", None, "tile", None),),
        out_specs=(P(None, None, "tile", "frame"), P()),
        check_vma=False,
    )
```

profile of v0, /device:TPU:2, one launch (start us, length us, event | category | flops | bytes accessed | tf_op | source)
XLA Modules:
  0.0 526.9 jit_solution(18431249091505621572)
XLA Ops:
  7.2 1.8 copy.46
  9.0 1.9 collective-permute-start
  10.9 5.8 %collective-permute-start.1 = (bf16[64,2,1,4096]{3,0,2,1:T(8,128)(2,1)S(1)}, bf16[64,2,1,4096]{3,0,2,1:T(8,128)(2,1)S(1)}, u32[]{:S(2)}, u32[]{:S(2)}) collective-permute-start(bf16[64,2,1,4096]{3,0,2,1:T(8,128)(2,1)S(1)} %copy.46), channel_id=1, source_target_pairs={{1,0},{2,1},{3,2},{4,3},{5,4},{6,5},{7,6},{8,7},{9,8},{10,9},{11,1... | collective-permute-start | bytes 3145736 | tf_op jit(solution)/shard_map/ppermute | solution.py:16
  16.7 10.5 %collective-permute-done = bf16[64,2,1,4096]{3,0,2,1:T(8,128)(2,1)S(1)} collective-permute-done((bf16[64,2,1,4096]{3,0,2,1:T(8,128)(2,1)S(1)}, bf16[64,2,1,4096]{3,0,2,1:T(8,128)(2,1)S(1)}, u32[]{:S(2)}, u32[]{:S(2)}) %collective-permute-start) | collective-permute-done | bytes 1048608 | tf_op jit(solution)/shard_map/ppermute | solution.py:15
  27.2 1.8 collective-permute-done.1
  29.0 0.5 maximum_convert_fusion
  29.5 0.7 fusion.35
  30.3 1.5 select_select_fusion
  32.2 4.7 copy.49
  36.9 6.1 %reshape.243 = bf16[8,2,49152]{2,1,0:T(2,128)(2,1)S(1)} reshape(bf16[4096,1,3,64]{3,2,1,0:T(4,128)(2,1)} %bitcast.77) | data formatting | bytes 3145728
  43.0 48.1 %all_to_all.15 = bf16[8,2,49152]{2,1,0:T(2,128)(2,1)S(1)} all-to-all(bf16[8,2,49152]{2,1,0:T(2,128)(2,1)S(1)} %reshape.243), channel_id=1, replica_groups=mesh['frame'=8,'tile'=32] {'frame'}, dimensions={0} | all-to-all | bytes 3145728 | tf_op jit(solution)/shard_map/all_to_all | solution.py:55
  91.2 4.8 reshape.244
  96.0 4.8 copy.67
  100.8 1.4 copy.51
  102.1 0.5 copy.69
  102.7 2.0 fusion.36
  104.9 2.1 convert_element_type.26
  107.0 0.3 copy.54
  107.3 0.8 copy.70
  108.2 248.2 %all-reduce.3.cloned.1.call-done = f32[512,512]{0,1:T(8,128)} async-done(((f32[512,512]{0,1:T(8,128)}), f32[512,512]{0,1:T(8,128)}) %all-reduce.3.cloned.1.call-update) | async-done | bytes 1048592 | tf_op jit(solution)/shard_map/psum | solution.py:61
  356.4 1.6 copy.53
  358.3 11.7 %cholesky.104 = f32[128,128]{1,0:T(8,128)S(1)} custom-call(f32[128,128]{1,0:T(8,128)S(1)} %cholesky.266), custom_call_target="Cholesky" | custom-call | tf_op jit(solution)/shard_map/jit(cholesky)/cholesky | solution.py:62
  370.2 9.8 %custom-call.30 = f32[1,128,128]{1,2,0:T(8,128)S(1)} custom-call(f32[1,128,128]{2,1,0:T(8,128)S(1)} %get-tuple-element.45), custom_call_target="InvertDiagBlocksLowerTriangular" | custom-call | tf_op jit(solution)/shard_map/jit(cholesky)/cholesky | solution.py:62
  380.0 0.3 constant_dynamic-update-slice_fusion.3
  380.4 0.3 convolution_subtract_fusion.3
  380.7 11.8 %cholesky.217 = f32[128,128]{1,0:T(8,128)S(1)} custom-call(f32[128,128]{1,0:T(8,128)S(1)} %cholesky.270), custom_call_target="Cholesky" | custom-call | tf_op jit(solution)/shard_map/jit(cholesky)/cholesky | solution.py:62
  392.6 0.6 compare_reduce_fusion.2
  393.2 0.6 compare_reduce_fusion.3
  393.8 9.8 %custom-call.31 = f32[1,128,128]{1,2,0:T(8,128)S(1)} custom-call(f32[1,128,128]{2,1,0:T(8,128)S(1)} %get-tuple-element.42), custom_call_target="InvertDiagBlocksLowerTriangular" | custom-call | tf_op jit(solution)/shard_map/jit(cholesky)/cholesky | solution.py:62
  403.6 0.3 convolution_dynamic-update-slice_fusion
  403.9 0.4 convolution_subtract_fusion.4
  404.3 11.7 %cholesky.238 = f32[128,128]{1,0:T(8,128)S(1)} custom-call(f32[128,128]{1,0:T(8,128)S(1)} %cholesky.275), custom_call_target="Cholesky" | custom-call | tf_op jit(solution)/shard_map/jit(cholesky)/cholesky | solution.py:62
  416.1 0.7 compare_reduce_fusion.1
  416.7 9.8 %custom-call.32 = f32[1,128,128]{1,2,0:T(8,128)S(1)} custom-call(f32[1,128,128]{2,1,0:T(8,128)S(1)} %get-tuple-element.39), custom_call_target="InvertDiagBlocksLowerTriangular" | custom-call | tf_op jit(solution)/shard_map/jit(cholesky)/cholesky | solution.py:62
  426.7 0.4 convolution_subtract_fusion.5
  427.1 11.9 %cholesky.255 = f32[128,128]{1,0:T(8,128)S(1)} custom-call(f32[128,128]{1,0:T(8,128)S(1)} %convolution_subtract_fusion.5), custom_call_target="Cholesky" | custom-call | tf_op jit(solution)/shard_map/jit(cholesky)/cholesky | solution.py:62
  439.1 0.7 compare_reduce_fusion
  442.3 0.3 multiply_bitcast_fusion
  442.6 10.0 %while.1 = (s32[]{:T(128)}, f32[512,512]{1,0:T(8,128)S(1)}, s32[4,2]{0,1:T(2,128)S(1)}, f32[4,128,128]{2,1,0:T(8,128)}, s32[]{:T(128)}) while((s32[]{:T(128)}, f32[512,512]{1,0:T(8,128)S(1)}, s32[4,2]{0,1:T(2,128)S(1)}, f32[4,128,128]{2,1,0:T(8,128)}, s32[]{:T(128)}) %tuple.39), condition=%wide.while_cond, body=%wide.while_body.sunk | while | flops 2 | bytes 132705 | solution.py:64
  442.7 0.5 fusion.46
  443.2 1.9 bitcast_dynamic-update-slice_fusion.2
  445.2 0.5 fusion.46
  445.7 1.9 bitcast_dynamic-update-slice_fusion.2
  447.7 0.5 fusion.46
  448.2 1.9 bitcast_dynamic-update-slice_fusion.2
  450.2 0.5 fusion.46
  450.7 1.9 bitcast_dynamic-update-slice_fusion.2
  452.6 40.2 %custom-call.33 = f32[4,128,128]{1,2,0:T(8,128)S(1)} custom-call(f32[4,128,128]{2,1,0:T(8,128)} %get-tuple-element.9), custom_call_target="InvertDiagBlocksLowerTriangular" | custom-call | tf_op jit(solution)/shard_map/triangular_solve | solution.py:64
  492.8 1.6 fusion.26
  494.4 2.1 convolution_subtract_fusion.2
  496.5 1.7 fusion.25
  498.3 1.9 convolution_subtract_fusion
  500.2 1.7 fusion.23
  501.9 3.4 fusion.1
  505.3 1.1 copy.57
  506.4 1.2 copy.56
  507.6 1.1 copy.55
  508.7 1.4 copy.58
  510.1 1.7 convolution_bitcast_fusion
  511.8 0.3 copy.62
  512.1 1.4 copy.61
  513.5 2.3 copy.60
  515.8 1.3 copy.64
  517.1 2.7 fusion.7
  (36 shorter events, 1.8 us)
Async XLA Ops:
  7.2 349.3 %all-reduce.3.cloned.1.call-start = ((), (), s32[]{:S(2)}) async-start(), calls=%async_computation.1 | async-start | bytes 2097152 | tf_op jit(solution)/shard_map/psum | solution.py:61
  9.0 18.2 %collective-permute-start = (bf16[64,2,1,4096]{3,0,2,1:T(8,128)(2,1)S(1)}, bf16[64,2,1,4096]{3,0,2,1:T(8,128)(2,1)S(1)}, u32[]{:S(2)}, u32[]{:S(2)}) collective-permute-start(bf16[64,2,1,4096]{3,0,2,1:T(8,128)(2,1)S(1)} %copy.46), channel_id=1, source_target_pairs={{0,1},{1,2},{2,3},{3,4},{4,5},{5,6},{6,7},{7,8},{8,9},{9,10},{10,1... | collective-permute-start | bytes 3145736 | tf_op jit(solution)/shard_map/ppermute | solution.py:15
  10.9 18.1 %collective-permute-start.1 = (bf16[64,2,1,4096]{3,0,2,1:T(8,128)(2,1)S(1)}, bf16[64,2,1,4096]{3,0,2,1:T(8,128)(2,1)S(1)}, u32[]{:S(2)}, u32[]{:S(2)}) collective-permute-start(bf16[64,2,1,4096]{3,0,2,1:T(8,128)(2,1)S(1)} %copy.46), channel_id=1, source_target_pairs={{1,0},{2,1},{3,2},{4,3},{5,4},{6,5},{7,6},{8,7},{9,8},{10,9},{11,1... | collective-permute-start | bytes 3145736 | tf_op jit(solution)/shard_map/ppermute | solution.py:16
  356.4 1.7 copy-start.1
  452.6 40.2 %copy-start.3 = (f32[512,512]{1,0:T(8,128)}, f32[512,512]{1,0:T(8,128)S(1)}, u32[]{:S(2)}) copy-start(f32[512,512]{1,0:T(8,128)S(1)} %get-tuple-element.100) | copy-start | bytes 3145732
  492.8 1.6 copy-start.4
  494.4 3.8 copy-start
  507.6 4.3 copy-start.2
Sparse Core Ops, SparseCore 0:
  104.8 251.5 all-reduce.2
where the time goes:
time: 532 us; the launch traced here: 527 us
  waiting for transfers between devices  261 us (49%)
  other arithmetic  127 us (24%)
  local copies, waits for them, and re-layouts  48.3 us (9%)
  blocking collectives  48.1 us (9%)
  matrix products  17.9 us (3%)
  between operations  17.2 us (3%)
  starting transfers between devices  7.71 us (1%)
    psum x1, waiting for transfers between devices, local(): gram = lax.psum(local_gram, ('frame', 'tile'))  248 us
    another operation x15, other arithmetic, local(): lower = jnp.linalg.cholesky(gram)  79.4 us
    all_to_all x1, blocking collectives, local(): lax.all_to_all(strain, 'frame', split_axis=3, concat_axis=0, tiled=True)  48.1 us
    another operation x2, other arithmetic, local(): lax.linalg.triangular_solve(lower, snapshot, left_side=True, lower=True)  40.2 us
    unnamed x16, local copies, waits for them, and re-layouts  15.4 us
    another operation x7, matrix products, local(): lax.linalg.triangular_solve(lower, snapshot, left_side=True, lower=True)  14.1 us
  transfers between devices with their start and end apart: 3, of which 3 were waited for; matrix products, arithmetic and copies ran while one was open for 1% of the time, Pallas kernels for 0%

commit v1 on v0

--- a/solution.py
+++ b/solution.py
@@ -52,7 +52,10 @@
     d_rows = derivative(center, field[:, :, :-2, :], field[:, :, 2:, :], first, final)
     d_cols = column_derivative(center)
     strain = combine_strain(d_rows, d_cols)
-    pixel_major = lax.all_to_all(strain, "frame", split_axis=3, concat_axis=0, tiled=True)
+    pixel_major = jnp.concatenate(
+        lax.all_to_all(jnp.stack(jnp.split(strain, lax.axis_size("frame"), axis=3)), "frame", 0, 0),
+        axis=0,
+    )
     frames = pixel_major.shape[0]
     snapshot_half = pixel_major.reshape(frames, -1)
     local_gram = lax.dot_general(

time: 532 us -> 510 us (0.959)
  local copies, waits for them, and re-layouts: 48.3 us -> 27.2 us
    unnamed x16 -> x21, local copies, waits for them, and re-layouts: 15.4 us -> 4.04 us
where the time goes in v1:
time: 510 us; the launch traced here: 506 us
  waiting for transfers between devices  262 us (51%)
  other arithmetic  127 us (25%)
  blocking collectives  48.1 us (9%)
  local copies, waits for them, and re-layouts  27.2 us (5%)
  between operations  17.2 us (3%)
  matrix products  16.8 us (3%)
  starting transfers between devices  7.71 us (2%)
    psum x1, waiting for transfers between devices, local(): gram = lax.psum(local_gram, ('frame', 'tile'))  249 us
    another operation x15, other arithmetic, local(): lower = jnp.linalg.cholesky(gram)  79.4 us
    all_to_all x1, blocking collectives, local(): lax.all_to_all(jnp.stack(jnp.split(strain, lax.axis_size('frame'), axis=3...  48.1 us
    another operation x2, other arithmetic, local(): lax.linalg.triangular_solve(lower, snapshot, left_side=True, lower=True)  40.2 us
    another operation x7, matrix products, local(): lax.linalg.triangular_solve(lower, snapshot, left_side=True, lower=True)  12.9 us
    ppermute x1, waiting for transfers between devices, with_halo(): before = lax.ppermute(last, axis, up)  10.5 us
  transfers between devices with their start and end apart: 3, of which 3 were waited for; matrix products, arithmetic and copies ran while one was open for 1% of the time, Pallas kernels for 0%

profile of v1, /device:TPU:2, one launch (start us, length us, event | category | flops | bytes accessed | tf_op | source)
XLA Modules:
  0.0 505.9 jit_solution(11377246017575653846)
XLA Ops:
  7.2 1.8 copy.38
  9.0 1.9 collective-permute-start
  10.9 5.8 %collective-permute-start.1 = (bf16[64,2,1,4096]{3,0,1,2:T(8,128)(2,1)S(1)}, bf16[64,2,1,4096]{3,0,1,2:T(8,128)(2,1)S(1)}, u32[]{:S(2)}, u32[]{:S(2)}) collective-permute-start(bf16[64,2,1,4096]{3,0,1,2:T(8,128)(2,1)S(1)} %copy.38), channel_id=1, source_target_pairs={{1,0},{2,1},{3,2},{4,3},{5,4},{6,5},{7,6},{8,7},{9,8},{10,9},{11,1... | collective-permute-start | bytes 3145736 | tf_op jit(solution)/shard_map/ppermute | solution.py:16
  16.7 10.5 %collective-permute-done = bf16[64,2,1,4096]{3,0,1,2:T(8,128)(2,1)S(1)} collective-permute-done((bf16[64,2,1,4096]{3,0,1,2:T(8,128)(2,1)S(1)}, bf16[64,2,1,4096]{3,0,1,2:T(8,128)(2,1)S(1)}, u32[]{:S(2)}, u32[]{:S(2)}) %collective-permute-start) | collective-permute-done | bytes 1048608 | tf_op jit(solution)/shard_map/ppermute | solution.py:15
  27.2 1.8 collective-permute-done.1
  29.0 0.5 maximum_convert_fusion
  29.5 0.7 fusion.43
  30.3 1.5 select_select_fusion
  32.0 0.2 pad_maximum_fusion.2
  32.4 48.1 %all_to_all.5 = bf16[8,64,3,1,512]{4,1,3,2,0:T(8,128)(2,1)S(1)} all-to-all(bf16[8,64,3,1,512]{4,1,3,2,0:T(8,128)(2,1)S(1)} %fusion.20), channel_id=1, replica_groups=mesh['frame'=8,'tile'=32] {'frame'}, dimensions={0} | all-to-all | bytes 3145728 | tf_op jit(solution)/shard_map/all_to_all | solution.py:56
  80.5 1.4 copy.48
  81.9 0.5 copy.65
  82.4 2.0 fusion.44
  84.4 2.1 convert_element_type.26
  86.5 0.3 copy.51
  87.0 249.3 %all-reduce.3.cloned.1.call-done = f32[512,512]{0,1:T(8,128)} async-done(((f32[512,512]{0,1:T(8,128)}), f32[512,512]{0,1:T(8,128)}) %all-reduce.3.cloned.1.call-update) | async-done | bytes 1048592 | tf_op jit(solution)/shard_map/psum | solution.py:64
  336.3 1.6 copy.50
  338.0 0.2 fusion.13
  338.2 11.7 %cholesky.104 = f32[128,128]{1,0:T(8,128)S(1)} custom-call(f32[128,128]{1,0:T(8,128)S(1)} %cholesky.266), custom_call_target="Cholesky" | custom-call | tf_op jit(solution)/shard_map/jit(cholesky)/cholesky | solution.py:65
  350.0 0.1 cholesky.224
  350.1 9.8 %custom-call.30 = f32[1,128,128]{1,2,0:T(8,128)S(1)} custom-call(f32[1,128,128]{2,1,0:T(8,128)S(1)} %get-tuple-element.43), custom_call_target="InvertDiagBlocksLowerTriangular" | custom-call | tf_op jit(solution)/shard_map/jit(cholesky)/cholesky | solution.py:65
  359.9 0.3 constant_dynamic-update-slice_fusion.3
  360.2 0.3 convolution_subtract_fusion.3
  360.6 11.9 %cholesky.217 = f32[128,128]{1,0:T(8,128)S(1)} custom-call(f32[128,128]{1,0:T(8,128)S(1)} %cholesky.270), custom_call_target="Cholesky" | custom-call | tf_op jit(solution)/shard_map/jit(cholesky)/cholesky | solution.py:65
  372.5 0.6 compare_reduce_fusion.2
  373.1 0.6 compare_reduce_fusion.3
  373.8 9.8 %custom-call.31 = f32[1,128,128]{1,2,0:T(8,128)S(1)} custom-call(f32[1,128,128]{2,1,0:T(8,128)S(1)} %get-tuple-element.40), custom_call_target="InvertDiagBlocksLowerTriangular" | custom-call | tf_op jit(solution)/shard_map/jit(cholesky)/cholesky | solution.py:65
  383.6 0.3 convolution_dynamic-update-slice_fusion
  383.8 0.4 convolution_subtract_fusion.4
  384.2 11.7 %cholesky.238 = f32[128,128]{1,0:T(8,128)S(1)} custom-call(f32[128,128]{1,0:T(8,128)S(1)} %cholesky.275), custom_call_target="Cholesky" | custom-call | tf_op jit(solution)/shard_map/jit(cholesky)/cholesky | solution.py:65
  396.0 0.7 compare_reduce_fusion.1
  396.6 9.8 %custom-call.32 = f32[1,128,128]{1,2,0:T(8,128)S(1)} custom-call(f32[1,128,128]{2,1,0:T(8,128)S(1)} %get-tuple-element.37), custom_call_target="InvertDiagBlocksLowerTriangular" | custom-call | tf_op jit(solution)/shard_map/jit(cholesky)/cholesky | solution.py:65
  406.4 0.2 convolution_dynamic-update-slice_fusion.1
  406.7 0.4 convolution_subtract_fusion.5
  407.0 11.9 %cholesky.255 = f32[128,128]{1,0:T(8,128)S(1)} custom-call(f32[128,128]{1,0:T(8,128)S(1)} %convolution_subtract_fusion.5), custom_call_target="Cholesky" | custom-call | tf_op jit(solution)/shard_map/jit(cholesky)/cholesky | solution.py:65
  419.0 0.7 compare_reduce_fusion
  422.2 0.3 multiply_bitcast_fusion
  422.5 10.0 %while.1 = (s32[]{:T(128)}, f32[512,512]{1,0:T(8,128)S(1)}, s32[4,2]{0,1:T(2,128)S(1)}, f32[4,128,128]{2,1,0:T(8,128)}, s32[]{:T(128)}) while((s32[]{:T(128)}, f32[512,512]{1,0:T(8,128)S(1)}, s32[4,2]{0,1:T(2,128)S(1)}, f32[4,128,128]{2,1,0:T(8,128)}, s32[]{:T(128)}) %tuple.38), condition=%wide.while_cond, body=%wide.while_body.sunk | while | flops 2 | bytes 132705 | solution.py:67
  422.6 0.5 fusion.54
  423.1 1.9 bitcast_dynamic-update-slice_fusion.2
  425.1 0.5 fusion.54
  425.6 1.9 bitcast_dynamic-update-slice_fusion.2
  427.6 0.5 fusion.54
  428.1 1.9 bitcast_dynamic-update-slice_fusion.2
  430.1 0.5 fusion.54
  430.6 1.9 bitcast_dynamic-update-slice_fusion.2
  432.5 40.2 %custom-call.33 = f32[4,128,128]{1,2,0:T(8,128)S(1)} custom-call(f32[4,128,128]{2,1,0:T(8,128)} %get-tuple-element.9), custom_call_target="InvertDiagBlocksLowerTriangular" | custom-call | tf_op jit(solution)/shard_map/triangular_solve | solution.py:67
  472.7 0.5 fusion.34
  473.3 0.2 copy-done.4
  473.4 2.1 convolution_subtract_fusion.2
  475.5 1.7 fusion.33
  477.2 1.9 convolution_subtract_fusion
  479.1 1.7 fusion.31
  480.8 3.4 fusion.1
  484.2 1.1 copy.54
  485.4 1.2 copy.53
  486.5 1.1 copy.52
  487.7 1.4 copy.55
  489.1 1.7 convolution_bitcast_fusion
  490.8 0.3 copy.59
  491.1 1.4 copy.58
  492.5 2.3 copy.57
  494.8 1.3 copy.61
  496.1 2.7 fusion.7
  (40 shorter events, 1.1 us)
Async XLA Ops:
  7.2 329.2 %all-reduce.3.cloned.1.call-start = ((), (), s32[]{:S(2)}) async-start(), calls=%async_computation.1 | async-start | bytes 2097152 | tf_op jit(solution)/shard_map/psum | solution.py:64
  9.0 18.2 %collective-permute-start = (bf16[64,2,1,4096]{3,0,1,2:T(8,128)(2,1)S(1)}, bf16[64,2,1,4096]{3,0,1,2:T(8,128)(2,1)S(1)}, u32[]{:S(2)}, u32[]{:S(2)}) collective-permute-start(bf16[64,2,1,4096]{3,0,1,2:T(8,128)(2,1)S(1)} %copy.38), channel_id=1, source_target_pairs={{0,1},{1,2},{2,3},{3,4},{4,5},{5,6},{6,7},{7,8},{8,9},{9,10},{10,1... | collective-permute-start | bytes 3145736 | tf_op jit(solution)/shard_map/ppermute | solution.py:15
  10.9 18.1 %collective-permute-start.1 = (bf16[64,2,1,4096]{3,0,1,2:T(8,128)(2,1)S(1)}, bf16[64,2,1,4096]{3,0,1,2:T(8,128)(2,1)S(1)}, u32[]{:S(2)}, u32[]{:S(2)}) collective-permute-start(bf16[64,2,1,4096]{3,0,1,2:T(8,128)(2,1)S(1)} %copy.38), channel_id=1, source_target_pairs={{1,0},{2,1},{3,2},{4,3},{5,4},{6,5},{7,6},{8,7},{9,8},{10,9},{11,1... | collective-permute-start | bytes 3145736 | tf_op jit(solution)/shard_map/ppermute | solution.py:16
  336.3 1.7 copy-start.1
  432.5 40.7 %copy-start.3 = (f32[512,512]{1,0:T(8,128)}, f32[512,512]{1,0:T(8,128)S(1)}, u32[]{:S(2)}) copy-start(f32[512,512]{1,0:T(8,128)S(1)} %get-tuple-element.98) | copy-start | bytes 3145732
  472.7 0.7 copy-start.4
  473.4 3.8 copy-start
  486.5 4.3 copy-start.2
Sparse Core Ops, SparseCore 0:
  84.5 251.7 all-reduce.2
